TPU v7x, 32 devices: a whole 2x2x4 slice. The times are simulated.
32 devices in a mesh: dp: 4 (over x, core), expert: 8 (over z, y).
Axes of the slice: x: 2, y: 2, z: 4, core: 2. Of those that a mesh axis runs over, the one named last changes fastest.
Arguments:
- tokens: bfloat16 [4096, 2048], P(('dp', 'expert')), may hold values from -6 to 6
- cotangent: bfloat16 [4096, 2048], P(('dp', 'expert')), may hold values from -6 to 6
- routes: int32 [4096, 3], P(('dp', 'expert')), may hold values from 0 to 7, all different within a row; in each aligned block of 128 rows (0 to 127, 128 to 255, ...) at most 60 rows name the same one
- gates: float32 [4096, 3], P(('dp', 'expert')), may hold values from 0.1 to 1
- gate_proj: bfloat16 [8, 768, 2048], P('expert'), may hold values from -0.125 to 0.125
- up_proj: bfloat16 [8, 768, 2048], P('expert'), may hold values from -0.125 to 0.125
- down_proj: bfloat16 [8, 768, 2048], P('expert'), may hold values from -0.21875 to 0.21875
Outputs:
- grad_tokens: bfloat16 [4096, 2048], P(('dp', 'expert'))
- grad_gate: bfloat16 [8, 768, 2048], P('expert', 'dp')
- grad_up: bfloat16 [8, 768, 2048], P('expert', 'dp')
- grad_down: bfloat16 [8, 768, 2048], P('expert', 'dp')
Inputs may be any that keep to these rules, and one draw needn't show every extreme that they name: `routes`: each row names 3 different experts. Among the 128 rows of one device, no expert is named more than 60 times, and in some devices' rows some expert is named exactly 60 times.
All inputs are finite; a program needn't handle non-finite values.
Results may differ from a plain program's by a relative error of at most 0.0089.
Values may be sent and summed in bfloat16 or wider, within the bound.
A program may use at most 128 MiB of HBM per device.

v0:
```python
import jax
import jax.numpy as jnp
from jax import lax
from jax.sharding import PartitionSpec as P


def expert_pass(rows_in, rows_grad, w_gate, w_up, w_down):
    gate_pre = jnp.einsum("rd,fd->rf", rows_in, w_gate, preferred_element_type=jnp.float32)
    up_pre = jnp.einsum("rd,fd->rf", rows_in, w_up, preferred_element_type=jnp.float32)
    sigma = jax.nn.sigmoid(gate_pre)
    active = gate_pre * sigma
    hidden = (active * up_pre).astype(jnp.bfloat16)
    grad_down = jnp.einsum("rf,rd->fd", hidden, rows_grad, preferred_element_type=jnp.float32)
    d_hidden = jnp.einsum("rd,fd->rf", rows_grad, w_down, preferred_element_type=jnp.float32)
    d_up = (d_hidden * active).astype(jnp.bfloat16)
    d_gate = (d_hidden * up_pre * sigma * (1.0 + gate_pre * (1.0 - sigma))).astype(jnp.bfloat16)
    grad_gate = jnp.einsum("rf,rd->fd", d_gate, rows_in, preferred_element_type=jnp.float32)
    grad_up = jnp.einsum("rf,rd->fd", d_up, rows_in, preferred_element_type=jnp.float32)
    d_assign = jnp.dot(d_gate, w_gate, preferred_element_type=jnp.float32) + jnp.dot(
        d_up, w_up, preferred_element_type=jnp.float32
    )
    return (d_assign, grad_gate, grad_up, grad_down)


def shards(tokens, cotangent, routes, gates, gate_proj, up_proj, down_proj):
    experts = lax.axis_size("expert")
    tok_count = tokens.shape[0]
    feature = tokens.shape[1]
    chosen = routes.shape[1]
    capacity = max(2, min(tok_count, 5 * tok_count * chosen // (4 * experts)))
    routes_flat = routes.reshape(-1)
    onehot = (routes_flat[:, None] == jnp.arange(experts, dtype=jnp.int32)[None, :]).astype(
        jnp.int32
    )
    slot_index = jnp.sum((jnp.cumsum(onehot, axis=0) - onehot) * onehot, axis=1)
    target = routes_flat * capacity + slot_index
    placing = (jnp.arange(experts * capacity, dtype=jnp.int32)[:, None] == target[None, :]).astype(
        jnp.bfloat16
    )
    scaled = (
        gates.reshape(-1)[:, None] * jnp.repeat(cotangent, chosen, axis=0).astype(jnp.float32)
    ).astype(jnp.bfloat16)
    stacked = jnp.concatenate([jnp.repeat(tokens, chosen, axis=0), scaled], axis=1)
    packed = jnp.dot(placing, stacked, preferred_element_type=jnp.float32).astype(jnp.bfloat16)
    sent_tokens = packed[:, :feature].reshape(experts, capacity, feature)
    sent_grads = packed[:, feature:].reshape(experts, capacity, feature)
    arrived = (
        lax.all_to_all(sent_tokens, "expert", split_axis=0, concat_axis=0, tiled=True),
        lax.all_to_all(sent_grads, "expert", split_axis=0, concat_axis=0, tiled=True),
    )
    d_assign, whole_gate, whole_up, whole_down = expert_pass(
        arrived[0].reshape(-1, feature),
        arrived[1].reshape(-1, feature),
        gate_proj[0],
        up_proj[0],
        down_proj[0],
    )
    reduced = d_assign.reshape(experts, capacity, feature)
    grad_gate, grad_up, grad_down = (
        lax.psum_scatter(whole_gate, "dp", scatter_dimension=0, tiled=True),
        lax.psum_scatter(whole_up, "dp", scatter_dimension=0, tiled=True),
        lax.psum_scatter(whole_down, "dp", scatter_dimension=0, tiled=True),
    )
    summed = lax.all_to_all(reduced, "expert", split_axis=0, concat_axis=0, tiled=True)
    picked = jnp.take(summed.reshape(experts * capacity, feature), target, axis=0)
    grad_tokens = jnp.sum(picked.reshape(tok_count, chosen, feature), axis=1).astype(jnp.bfloat16)
    return (
        grad_tokens,
        grad_gate.astype(jnp.bfloat16)[None],
        grad_up.astype(jnp.bfloat16)[None],
        grad_down.astype(jnp.bfloat16)[None],
    )


def solution(mesh):
    return jax.shard_map(
        shards,
        mesh=mesh,
        in_specs=(
            P(("dp", "expert"), None),
            P(("dp", "expert"), None),
            P(("dp", "expert"), None),
            P(("dp", "expert"), None),
            P("expert", None, None),
            P("expert", None, None),
            P("expert", None, None),
        ),
        out_specs=(
            P(("dp", "expert"), None),
            P("expert", "dp", None),
            P("expert", "dp", None),
            P("expert", "dp", None),
        ),
        check_vma=False,
    )
```

profile of v0, /device:TPU:0, one launch (start us, length us, event | category | flops | bytes accessed | tf_op | source)
XLA Modules:
  0.0 346.3 jit_solution(12083527421723551145)
XLA Ops:
  10.8 3.4 broadcast_in_dim.29
  14.2 5.0 %reshape.104 = bf16[384,2048]{1,0:T(8,128)(2,1)} reshape(bf16[128,3,2048]{2,1,0:T(4,128)(2,1)} %broadcast_in_dim.29) | data formatting | bytes 3145728 | tf_op jit(solution)/shard_map/reshape | solution.py:43
  19.2 4.2 %broadcast_in_dim.30 = f32[128,3,2048]{2,1,0:T(4,128)} broadcast(bf16[128,2048]{1,0:T(8,128)(2,1)} %param.8), dimensions={0,2} | broadcast | bytes 3670016 | tf_op jit(solution)/shard_map/broadcast_in_dim | solution.py:41
  23.4 6.0 %convert_element_type.45 = f32[384,2048]{1,0:T(8,128)} reshape(f32[128,3,2048]{2,1,0:T(4,128)} %broadcast_in_dim.30) | data formatting | bytes 6291456 | tf_op jit(solution)/shard_map/convert_element_type | solution.py:41
  34.0 2.2 fusion.26
  36.2 2.7 reshape.107
  38.9 7.3 %all-to-all-start.1 = ((bf16[8,60,2048]{2,1,0:T(8,128)(2,1)}), bf16[8,60,2048]{2,1,0:T(8,128)(2,1)}, u32[]{:S(2)}, u32[]{:S(2)}) async-start(bf16[8,60,2048]{2,1,0:T(8,128)(2,1)} %reshape.107), calls=%async_computation.1 | async-start | bytes 4194304 | tf_op jit(solution)/shard_map/all_to_all | solution.py:48
  46.2 2.7 reshape.105
  49.0 45.6 %all-to-all-done.1 = bf16[8,60,2048]{2,1,0:T(8,128)(2,1)} async-done(((bf16[8,60,2048]{2,1,0:T(8,128)(2,1)}), bf16[8,60,2048]{2,1,0:T(8,128)(2,1)}, u32[]{:S(2)}, u32[]{:S(2)}) %all-to-all-start.1) | async-done | bytes 1966112 | tf_op jit(solution)/shard_map/all_to_all | solution.py:48
  94.6 4.4 %all-to-all-start = ((bf16[8,60,2048]{2,1,0:T(8,128)(2,1)}), bf16[8,60,2048]{2,1,0:T(8,128)(2,1)}, u32[]{:S(2)}, u32[]{:S(2)}) async-start(bf16[8,60,2048]{2,1,0:T(8,128)(2,1)} %reshape.105), calls=%async_computation | async-start | bytes 4194304 | tf_op jit(solution)/shard_map/all_to_all | solution.py:49
  99.0 2.7 reshape.108
  101.8 4.6 %fusion.5 = f32[480,768]{1,0:T(8,128)} fusion(bf16[480,2048]{1,0:T(8,128)(2,1)} %reshape.108, bf16[1,768,2048]{2,1,0:T(8,128)(2,1)S(1)} %copy-done), kind=kOutput, calls=%fused_computation.8 | convolution fusion | flops 1509949440 | bytes 6586368 | tf_op jit(solution)/shard_map/rd,fd->rf/dot_general | solution.py:8
  106.4 2.8 fusion.9
  109.2 37.5 %all-to-all-done = bf16[8,60,2048]{2,1,0:T(8,128)(2,1)} async-done(((bf16[8,60,2048]{2,1,0:T(8,128)(2,1)}), bf16[8,60,2048]{2,1,0:T(8,128)(2,1)}, u32[]{:S(2)}, u32[]{:S(2)}) %all-to-all-start) | async-done | bytes 1966112 | tf_op jit(solution)/shard_map/all_to_all | solution.py:49
  146.8 2.7 reshape.106
  149.5 7.0 %fusion.17 = f32[768,2048]{1,0:T(8,128)} fusion(bf16[480,2048]{1,0:T(8,128)(2,1)} %reshape.106, f32[480,768]{1,0:T(8,128)} %fusion.9, f32[480,768]{1,0:T(8,128)} %fusion.5), kind=kOutput, calls=%fused_computation.26 | convolution fusion | flops 1512161280 | bytes 11206656 | tf_op jit(solution)/shard_map/rf,rd->fd/dot_general | solution.py:13
  156.7 6.4 %multiply_convert_fusion.2 = (bf16[480,768]{1,0:T(8,128)(2,1)S(1)}, bf16[480,768]{1,0:T(8,128)(2,1)}) fusion(f32[480,768]{1,0:T(8,128)} %fusion.5, f32[480,768]{1,0:T(8,128)} %fusion.9, bf16[480,2048]{1,0:T(8,128)(2,1)} %reshape.106, bf16[1,768,2048]{2,1,0:T(8,128)(2,1)} %param.13), kind=kOutput, calls=%fused_computation.19 | convolution fusion | flops 1514741760 | bytes 9535488 | tf_op jit(solution)/shard_map/rd,fd->rf/dot_general | solution.py:14
  164.0 4.5 %fusion.28 = f32[768,2048]{1,0:T(8,128)} fusion(bf16[480,768]{1,0:T(8,128)(2,1)S(1)} %get-tuple-element.6, bf16[480,2048]{1,0:T(8,128)(2,1)S(1)} %copy-done.2), kind=kOutput, calls=%fused_computation.47 | convolution fusion | flops 1509949440 | bytes 8994816 | tf_op jit(solution)/shard_map/rf,rd->fd/dot_general | solution.py:18
  168.6 6.4 %fusion.27 = f32[768,2048]{1,0:T(8,128)} fusion(bf16[480,768]{1,0:T(8,128)(2,1)} %get-tuple-element.7, bf16[480,2048]{1,0:T(8,128)(2,1)} %reshape.108), kind=kOutput, calls=%fused_computation.46 | convolution fusion | flops 1509949440 | bytes 8994816 | tf_op jit(solution)/shard_map/rf,rd->fd/dot_general | solution.py:17
  175.0 3.0 fusion.3
  178.0 3.7 %fusion.13 = f32[480,2048]{1,0:T(8,128)} fusion(f32[480,2048]{1,0:T(8,128)S(1)} %fusion.3, bf16[480,768]{1,0:T(8,128)(2,1)S(1)} %copy-done.4, bf16[1,768,2048]{2,1,0:T(8,128)(2,1)S(1)} %copy-done.6), kind=kOutput, calls=%fused_computation.17 | convolution fusion | flops 1510932480 | bytes 11747328 | tf_op jit(solution)/shard_map/dot_general | solution.py:19
  181.7 3.8 %reshape.109 = f32[8,60,2048]{2,1,0:T(8,128)} reshape(f32[480,2048]{1,0:T(8,128)} %fusion.13) | data formatting | bytes 7864320 | tf_op jit(solution)/shard_map/reshape | solution.py:58
  185.5 4.9 %all-to-all-start.2 = ((f32[8,60,2048]{2,1,0:T(8,128)}), f32[8,60,2048]{2,1,0:T(8,128)}, u32[]{:S(2)}, u32[]{:S(2)}) async-start(f32[8,60,2048]{2,1,0:T(8,128)} %reshape.109), calls=%async_computation.2 | async-start | bytes 8388608 | tf_op jit(solution)/shard_map/all_to_all | solution.py:64
  191.2 92.8 %all-to-all-done.2 = f32[8,60,2048]{2,1,0:T(8,128)} async-done(((f32[8,60,2048]{2,1,0:T(8,128)}), f32[8,60,2048]{2,1,0:T(8,128)}, u32[]{:S(2)}, u32[]{:S(2)}) %all-to-all-start.2) | async-done | bytes 3932192 | tf_op jit(solution)/shard_map/all_to_all | solution.py:64
  284.0 4.4 %reshape.110 = f32[480,2048]{1,0:T(8,128)} reshape(f32[8,60,2048]{2,1,0:T(8,128)} %all-to-all-done.2) | data formatting | bytes 7864320 | tf_op jit(solution)/shard_map/reshape | solution.py:65
  288.4 7.8 %gather_fusion = f32[384,2048]{1,0:T(8,128)} fusion(f32[480,2048]{1,0:T(8,128)} %reshape.110, s32[1024]{0:T(1024)S(1)} %pad_clamp_fusion), kind=kCustom, calls=%fused_computation | custom fusion | bytes 6292992 | tf_op jit(solution)/shard_map/jit(_take)/gather | solution.py:65
  296.2 6.0 %gather.7 = f32[128,3,2048]{2,1,0:T(4,128)} reshape(f32[384,2048]{1,0:T(8,128)} %gather_fusion) | data formatting | bytes 6291456 | tf_op jit(solution)/shard_map/jit(_take)/gather | solution.py:65
  302.2 6.3 %select_reduce_fusion = bf16[128,2048]{1,0:T(8,128)(2,1)} fusion(f32[128,3,2048]{2,1,0:T(4,128)} %gather.7, pred[128,3]{1,0:T(8,128)(4,1)S(1)} %copy.19), kind=kLoop, calls=%fused_computation.2 | loop fusion | flops 1310720 | bytes 3670400 | tf_op jit(solution)/shard_map/reduce_sum | solution.py:66
  308.5 2.4 convert_bitcast_fusion
  310.9 2.4 convert_bitcast_fusion.1
  313.4 24.0 %reduce-scatter.4.cloned.1.call-done = f32[192,2048]{1,0:T(8,128)} async-done(((f32[768,2048]{1,0:T(8,128)}), f32[192,2048]{1,0:T(8,128)}) %reduce-scatter.4.cloned.1.call-update) | async-done | bytes 1572880 | tf_op jit(solution)/shard_map/reduce_scatter | solution.py:60
  337.3 2.4 convert_bitcast_fusion.2
  (48 shorter events, 10.2 us)
Async XLA Ops:
  7.2 94.6 %copy-start = (bf16[1,768,2048]{2,1,0:T(8,128)(2,1)S(1)}, bf16[1,768,2048]{2,1,0:T(8,128)(2,1)}, u32[]{:S(2)}) copy-start(bf16[1,768,2048]{2,1,0:T(8,128)(2,1)} %param.11) | copy-start | bytes 9437188
  29.4 2.4 copy-start.7
  38.9 55.7 %all-to-all-start.1 = ((bf16[8,60,2048]{2,1,0:T(8,128)(2,1)}), bf16[8,60,2048]{2,1,0:T(8,128)(2,1)}, u32[]{:S(2)}, u32[]{:S(2)}) async-start(bf16[8,60,2048]{2,1,0:T(8,128)(2,1)} %reshape.107), calls=%async_computation.1 | async-start | bytes 4194304 | tf_op jit(solution)/shard_map/all_to_all | solution.py:48
  94.6 52.2 %all-to-all-start = ((bf16[8,60,2048]{2,1,0:T(8,128)(2,1)}), bf16[8,60,2048]{2,1,0:T(8,128)(2,1)}, u32[]{:S(2)}, u32[]{:S(2)}) async-start(bf16[8,60,2048]{2,1,0:T(8,128)(2,1)} %reshape.105), calls=%async_computation | async-start | bytes 4194304 | tf_op jit(solution)/shard_map/all_to_all | solution.py:49
  99.0 209.6 %reduce-scatter.8.cloned.1.call-start = ((), (), s32[]{:S(2)}) async-start(), calls=%async_computation.8 | async-start | bytes 7864320 | tf_op jit(solution)/shard_map/reduce_scatter | solution.py:62
  101.7 4.6 %copy-start.1 = (bf16[480,2048]{1,0:T(8,128)(2,1)S(1)}, bf16[480,2048]{1,0:T(8,128)(2,1)}, u32[]{:S(2)}) copy-start(bf16[480,2048]{1,0:T(8,128)(2,1)} %reshape.108) | copy-start | bytes 5898244
  101.7 4.6 %copy-start.5 = (bf16[1,768,2048]{2,1,0:T(8,128)(2,1)S(1)}, bf16[1,768,2048]{2,1,0:T(8,128)(2,1)}, u32[]{:S(2)}) copy-start(bf16[1,768,2048]{2,1,0:T(8,128)(2,1)} %param.12) | copy-start | bytes 9437188
  156.5 154.5 %reduce-scatter.6.cloned.1.call-start = ((), (), s32[]{:S(2)}) async-start(), calls=%async_computation.7 | async-start | bytes 7864320 | tf_op jit(solution)/shard_map/reduce_scatter | solution.py:61
  156.7 7.3 %copy-start.2 = (bf16[480,2048]{1,0:T(8,128)(2,1)S(1)}, bf16[480,2048]{1,0:T(8,128)(2,1)}, u32[]{:S(2)}) copy-start(bf16[480,2048]{1,0:T(8,128)(2,1)} %reshape.108) | copy-start | bytes 5898244
  163.1 0.9 copy-start.3
  168.6 168.7 %reduce-scatter.4.cloned.1.call-start = ((), (), s32[]{:S(2)}) async-start(), calls=%async_computation.6 | async-start | bytes 7864320 | tf_op jit(solution)/shard_map/reduce_scatter | solution.py:60
  175.0 3.0 copy-start.4
  175.0 3.0 copy-start.6
  185.5 5.1 %copy-start.8 = (s32[128,3]{0,1:T(4,128)S(1)}, s32[128,3]{0,1:T(4,128)}, u32[]{:S(2)}) copy-start(s32[128,3]{0,1:T(4,128)} %param.9) | copy-start | bytes 4612
  185.5 98.5 %all-to-all-start.2 = ((f32[8,60,2048]{2,1,0:T(8,128)}), f32[8,60,2048]{2,1,0:T(8,128)}, u32[]{:S(2)}, u32[]{:S(2)}) async-start(f32[8,60,2048]{2,1,0:T(8,128)} %reshape.109), calls=%async_computation.2 | async-start | bytes 8388608 | tf_op jit(solution)/shard_map/all_to_all | solution.py:64
Sparse Core Ops, SparseCore 0:
  156.6 57.8 reduce-scatter.7
  217.0 58.8 reduce-scatter.5
  278.4 58.8 reduce-scatter.3
where the time goes:
time: 347 us; the launch traced here: 346 us
  waiting for transfers between devices  200 us (58%)
  local copies, waits for them, and re-layouts  58.1 us (17%)
  matrix products  40.6 us (12%)
  starting transfers between devices  16.9 us (5%)
  other arithmetic  16.8 us (5%)
  between operations  13.9 us (4%)
    all_to_all x1, waiting for transfers between devices, shards(): lax.all_to_all(reduced, 'expert', split_axis=0, concat_axis=0, tiled=True)  92.8 us
    all_to_all x1, waiting for transfers between devices, shards(): lax.all_to_all(sent_tokens, 'expert', split_axis=0, concat_axis=0, tiled=...  45.6 us
    all_to_all x1, waiting for transfers between devices, shards(): lax.all_to_all(sent_grads, 'expert', split_axis=0, concat_axis=0, tiled=T...  37.5 us
    reduce_scatter x1, waiting for transfers between devices, shards(): lax.psum_scatter(whole_gate, 'dp', scatter_dimension=0, tiled=True)  24 us
    gather x2, local copies, waits for them, and re-layouts, shards(): jnp.take(summed.reshape(experts * capacity, feature), target, axis=0)  13.8 us
    all_to_all x1, starting transfers between devices, shards(): lax.all_to_all(sent_tokens, 'expert', split_axis=0, concat_axis=0, tiled=...  7.31 us
    dot_general x1, matrix products, expert_pass(): jnp.einsum('rf,rd->fd', hidden, rows_grad, preferred_element_type=jnp.flo...  6.97 us
  transfers between devices with their start and end apart: 6, of which 4 were waited for; matrix products, arithmetic and copies ran while one was open for 20% of the time, Pallas kernels for 0%

commit v1 on v0

--- a/solution.py
+++ b/solution.py
@@ -1,6 +1,10 @@
+import functools
+
 import jax
 import jax.numpy as jnp
 from jax import lax
+from jax.experimental import pallas as pl
+from jax.experimental.pallas import tpu as pltpu
 from jax.sharding import PartitionSpec as P
 
 
@@ -72,9 +76,282 @@
     )
 
 
+NT = (((1,), (1,)), ((), ()))
+TN = (((0,), (0,)), ((), ()))
+
+
+def flip(index, offset, count):
+    total, bit = 0, 1
+    while bit < count:
+        total = total + ((index // bit) % 2 + (offset // bit) % 2) % 2 * bit
+        bit *= 2
+    return total
+
+
+def layer_kernel(
+    experts, cap, group, tok_ref, grd_ref, wg_hbm, wu_hbm, wd_hbm,
+    ret_ref, og_ref, ou_ref, od_ref,
+    rows, grads, wg, wu, wd, gate, up, hid, dgate, dup, dass,
+    core_out, core_in, x_out, x_in, own,
+    w_sem, loc_sem, tok_s, tok_r, grd_s, grd_r, ret_s, ret_r, core_s, core_r, x_s, x_r,
+):
+    me = lax.axis_index("expert")
+    rank = lax.axis_index("dp")
+    half, side = rank // 2, rank % 2
+    core_peer = half * 2 + (1 - side)
+    x_peer = (1 - half) * 2 + side
+    ff, feature = wg.shape
+    share = ff // 4
+    f32, bf16 = jnp.float32, jnp.bfloat16
+
+    loads = [
+        pltpu.make_async_copy(a, b, w_sem.at[i])
+        for i, (a, b) in enumerate(((wg_hbm, wg), (wu_hbm, wu), (wd_hbm, wd)))
+    ]
+    for c in loads:
+        c.start()
+    mine = [
+        pltpu.make_async_copy(tok_ref.at[me], rows.at[pl.ds(0, cap)], loc_sem.at[0]),
+        pltpu.make_async_copy(grd_ref.at[me], grads.at[pl.ds(0, cap)], loc_sem.at[1]),
+    ]
+    for c in mine:
+        c.start()
+
+    barrier = pltpu.get_barrier_semaphore()
+    for d in range(1, experts):
+        pl.semaphore_signal(barrier, inc=1, device_id={"expert": flip(me, d, experts)}, device_id_type=pl.DeviceIdType.MESH)
+    for p in (core_peer, x_peer):
+        pl.semaphore_signal(barrier, inc=1, device_id={"dp": p}, device_id_type=pl.DeviceIdType.MESH)
+    pl.semaphore_wait(barrier, experts + 1)
+
+    def to_expert(src, dst, s, r, d):
+        return pltpu.make_async_remote_copy(
+            src_ref=src, dst_ref=dst, send_sem=s.at[d], recv_sem=r.at[d],
+            device_id={"expert": flip(me, d, experts)}, device_id_type=pl.DeviceIdType.MESH,
+        )
+
+    near = list(range(1, experts // 2))
+    far = list(range(experts // 2, experts))
+    tok_c, grd_c = {}, {}
+    for d in far + near:
+        tok_c[d] = to_expert(tok_ref.at[flip(me, d, experts)], rows.at[pl.ds(d * cap, cap)], tok_s, tok_r, d)
+        tok_c[d].start()
+    for d in near + far:
+        grd_c[d] = to_expert(grd_ref.at[flip(me, d, experts)], grads.at[pl.ds(d * cap, cap)], grd_s, grd_r, d)
+        grd_c[d].start()
+
+    tile = ff // 2
+
+    def forward(g):
+        span = pl.ds(g * group, group)
+
+        @pl.loop(0, 2)
+        def _(t):
+            part = pl.ds(pl.multiple_of(t * tile, tile), tile)
+            x = rows[span, :]
+            gp = lax.dot_general(wg[part, :], x, NT, preferred_element_type=f32)
+            u = lax.dot_general(wu[part, :], x, NT, preferred_element_type=f32)
+            gate[part, span] = gp
+            up[part, span] = u
+            hid[part, span] = (gp * jax.nn.sigmoid(gp) * u).astype(bf16)
+
+    def backward(g):
+        span = pl.ds(g * group, group)
+
+        @pl.loop(0, 2)
+        def _(t):
+            part = pl.ds(pl.multiple_of(t * tile, tile), tile)
+            dh = lax.dot_general(wd[part, :], grads[span, :], NT, preferred_element_type=f32)
+            gp = gate[part, span]
+            s = jax.nn.sigmoid(gp)
+            dup[part, span] = (dh * (gp * s)).astype(bf16)
+            dgate[part, span] = (dh * up[part, span] * s * (1.0 + gp * (1.0 - s))).astype(bf16)
+
+    wide = feature // 4
+
+    def assign(g):
+        span = pl.ds(g * group, group)
+
+        @pl.loop(0, 4)
+        def _(t):
+            cols = pl.ds(pl.multiple_of(t * wide, wide), wide)
+            v = lax.dot_general(dgate[:, span], wg[:, cols], TN, preferred_element_type=f32)
+            v += lax.dot_general(dup[:, span], wu[:, cols], TN, preferred_element_type=f32)
+            dass[span, cols] = v.astype(bf16)
+
+    def weight_grad(a, j, store):
+        left = (dgate, dup, hid)[a]
+        right = (rows, rows, grads)[a]
+        part = pl.ds(pl.multiple_of(j * share, share), share)
+
+        @pl.loop(0, 4)
+        def _(t):
+            cols = pl.ds(pl.multiple_of(t * wide, wide), wide)
+            store(cols, jnp.dot(left[part, :], right[:, cols], preferred_element_type=f32))
+
+    for c in loads[:2]:
+        c.wait()
+    mine[0].wait()
+    for d in near:
+        tok_c[d].wait_recv()
+    forward(0)
+    for d in far:
+        tok_c[d].wait_recv()
+    forward(1)
+    loads[2].wait()
+    mine[1].wait()
+    for d in near:
+        grd_c[d].wait_recv()
+    backward(0)
+    assign(0)
+    ret_c = {}
+    own_back = pltpu.make_async_copy(dass.at[pl.ds(0, cap)], ret_ref.at[me], loc_sem.at[0])
+    own_back.start()
+    for d in near:
+        ret_c[d] = to_expert(dass.at[pl.ds(d * cap, cap)], ret_ref.at[me], ret_s, ret_r, d)
+        ret_c[d].start()
+    for d in far:
+        grd_c[d].wait_recv()
+    backward(1)
+
+    core_c = {}
+
+    def send_core(k, a, j):
+        def store(cols, v):
+            core_out[k * 3 + a, :, cols] = v.astype(bf16)
+
+        weight_grad(a, j, store)
+        core_c[k, a] = pltpu.make_async_remote_copy(
+            src_ref=core_out.at[k * 3 + a], dst_ref=core_in.at[k * 3 + a],
+            send_sem=core_s.at[k * 3 + a], recv_sem=core_r.at[k * 3 + a],
+            device_id={"dp": core_peer}, device_id_type=pl.DeviceIdType.MESH,
+        )
+        core_c[k, a].start()
+
+    for a in range(3):
+        send_core(0, a, (1 - half) * 2 + (1 - side))
+    assign(1)
+    for d in far:
+        ret_c[d] = to_expert(dass.at[pl.ds(d * cap, cap)], ret_ref.at[me], ret_s, ret_r, d)
+        ret_c[d].start()
+    x_c = {}
+    for a in range(3):
+        core_c[0, a].wait_recv()
+
+        def store(cols, v, a=a):
+            x_out[a, :, cols] = (v + core_in[a, :, cols].astype(f32)).astype(bf16)
+
+        weight_grad(a, (1 - half) * 2 + side, store)
+        x_c[a] = pltpu.make_async_remote_copy(
+            src_ref=x_out.at[a], dst_ref=x_in.at[a], send_sem=x_s.at[a], recv_sem=x_r.at[a],
+            device_id={"dp": x_peer}, device_id_type=pl.DeviceIdType.MESH,
+        )
+        x_c[a].start()
+    for a in range(3):
+        send_core(1, a, half * 2 + (1 - side))
+    for a in range(3):
+        core_c[1, a].wait_recv()
+
+        def store(cols, v, a=a):
+            own[a, :, cols] = v + core_in[3 + a, :, cols].astype(f32)
+
+        weight_grad(a, half * 2 + side, store)
+    for a, out in enumerate((og_ref, ou_ref, od_ref)):
+        x_c[a].wait_recv()
+
+        @pl.loop(0, 4)
+        def _(t, a=a, out=out):
+            cols = pl.ds(pl.multiple_of(t * wide, wide), wide)
+            out[:, cols] = (own[a, :, cols] + x_in[a, :, cols].astype(f32)).astype(bf16)
+
+    own_back.wait()
+    for d in range(1, experts):
+        ret_c[d].wait_recv()
+        tok_c[d].wait_send()
+        grd_c[d].wait_send()
+        ret_c[d].wait_send()
+    for c in core_c.values():
+        c.wait_send()
+    for c in x_c.values():
+        c.wait_send()
+
+
+def gathered(tokens, cotangent, routes, gates, gate_proj, up_proj, down_proj):
+    experts = lax.axis_size("expert")
+    tok_count, feature = tokens.shape
+    chosen = routes.shape[1]
+    ff = gate_proj.shape[1]
+    capacity = max(2, min(tok_count, 5 * tok_count * chosen // (4 * experts)))
+    cap = -(-capacity // 16) * 16
+    f32, bf16 = jnp.float32, jnp.bfloat16
+    hit = routes[:, :, None] == jnp.arange(experts, dtype=jnp.int32)[None, None, :]
+    member = jnp.any(hit, axis=1)
+    weight = jnp.sum(jnp.where(hit, gates[:, :, None], 0.0), axis=1)
+    at = jnp.arange(tok_count, dtype=jnp.int32)
+    earlier = (at[None, :] < at[:, None]).astype(bf16)
+    slot = jnp.dot(earlier, member.astype(bf16), preferred_element_type=f32).astype(jnp.int32)
+    slot = jnp.where(member, slot, cap)
+    picks = slot.T[:, None, :] == jnp.arange(cap, dtype=jnp.int32)[None, :, None]
+    placing = picks.reshape(experts * cap, tok_count).astype(bf16)
+    factor = jnp.sum(jnp.where(picks, weight.T[:, None, :], 0.0), axis=2).reshape(-1, 1)
+    packed = jnp.dot(placing, tokens, preferred_element_type=f32).astype(bf16)
+    packed_grads = (factor * jnp.dot(placing, cotangent, preferred_element_type=f32)).astype(bf16)
+    group = experts * cap // 2
+    share = ff // 4
+    rows = experts * cap
+    vm = pl.BlockSpec(memory_space=pltpu.VMEM)
+    anyspec = pl.BlockSpec(memory_space=pl.ANY)
+    sem = pltpu.SemaphoreType.DMA
+    back, grad_gate, grad_up, grad_down = pl.pallas_call(
+        functools.partial(layer_kernel, experts, cap, group),
+        out_shape=[jax.ShapeDtypeStruct((experts, cap, feature), bf16)]
+        + [jax.ShapeDtypeStruct((share, feature), bf16)] * 3,
+        in_specs=[vm, vm, anyspec, anyspec, anyspec],
+        out_specs=[vm] * 4,
+        scratch_shapes=[
+            pltpu.VMEM((rows, feature), bf16),
+            pltpu.VMEM((rows, feature), bf16),
+            pltpu.VMEM((ff, feature), bf16),
+            pltpu.VMEM((ff, feature), bf16),
+            pltpu.VMEM((ff, feature), bf16),
+            pltpu.VMEM((ff, rows), f32),
+            pltpu.VMEM((ff, rows), f32),
+            pltpu.VMEM((ff, rows), bf16),
+            pltpu.VMEM((ff, rows), bf16),
+            pltpu.VMEM((ff, rows), bf16),
+            pltpu.VMEM((rows, feature), bf16),
+            pltpu.VMEM((6, share, feature), bf16),
+            pltpu.VMEM((6, share, feature), bf16),
+            pltpu.VMEM((3, share, feature), bf16),
+            pltpu.VMEM((3, share, feature), bf16),
+            pltpu.VMEM((3, share, feature), f32),
+            sem((3,)), sem((2,)),
+            sem((experts,)), sem((experts,)), sem((experts,)), sem((experts,)),
+            sem((experts,)), sem((experts,)),
+            sem((6,)), sem((6,)), sem((3,)), sem((3,)),
+        ],
+        compiler_params=pltpu.CompilerParams(
+            collective_id=0, has_side_effects=True, vmem_limit_bytes=64 * 1024 * 1024 - 65536
+        ),
+    )(
+        packed.reshape(experts, cap, feature),
+        packed_grads.reshape(experts, cap, feature),
+        gate_proj[0], up_proj[0], down_proj[0],
+    )
+    grad_tokens = lax.dot_general(
+        placing, back.reshape(rows, feature), TN, preferred_element_type=f32
+    ).astype(bf16)
+    return grad_tokens, grad_gate[None], grad_up[None], grad_down[None]
+
+
+def fits(mesh):
+    experts, replicas = mesh.shape["expert"], mesh.shape["dp"]
+    return replicas == 4 and experts & (experts - 1) == 0 and experts <= 2 * replicas
+
+
 def solution(mesh):
     return jax.shard_map(
-        shards,
+        gathered if fits(mesh) else shards,
         mesh=mesh,
         in_specs=(
             P(("dp", "expert"), None),

time: 347 us -> 200 us (0.58)
  the two profiles are of different devices: /device:TPU:0 before, /device:TPU:8 now
where the time goes in v1:
time: 200 us; the launch traced here: 199 us
  Pallas kernels  186 us (93%)
  matrix products  8.23 us (4%)
  local copies, waits for them, and re-layouts  2.82 us (1%)
    pallas_call x1, Pallas kernels, gathered(): pl.pallas_call(functools.partial(layer_kernel, experts, cap, group), out_...  186 us

profile of v1, /device:TPU:8, one launch (start us, length us, event | category | flops | bytes accessed | tf_op | source)
XLA Modules:
  0.0 199.3 jit_solution(15226978923568583383)
XLA Ops:
  0.6 0.0 copy-start.3
  0.6 0.7 fusion.3
  1.4 0.1 fusion.1
  1.5 0.0 copy-start.4
  1.5 0.7 select_reduce_fusion.1
  2.3 0.1 select_reduce_fusion
  2.4 0.1 mul.10
  2.5 0.1 eq.45
  2.6 0.1 bitcast_compare_fusion
  2.7 3.0 %multiply_convert_fusion = bf16[512,2048]{1,0:T(8,128)(2,1)} fusion(pred[512,128]{1,0:T(32,128)(4,1)S(1)} %bitcast_compare_fusion, bf16[128,2048]{1,0:T(8,128)(2,1)} %param.8, f32[512]{0:T(512)S(1)} %mul.10), kind=kOutput, calls=%fused_computation | convolution fusion | flops 270532608 | bytes 2689024 | tf_op jit(solution)/shard_map/dot_general | solution.py:298
  5.7 0.0 copy-done.3
  5.8 2.0 %convolution_convert_fusion = bf16[512,2048]{1,0:T(8,128)(2,1)} fusion(pred[512,128]{1,0:T(32,128)(4,1)S(1)} %bitcast_compare_fusion, bf16[128,2048]{1,0:T(8,128)(2,1)S(1)} %copy-done.3), kind=kOutput, calls=%fused_computation.1 | convolution fusion | flops 269484032 | bytes 2686976 | tf_op jit(solution)/shard_map/dot_general | solution.py:297
  7.8 0.0 copy-done.4
  7.8 185.8 %shard_map.102 = (bf16[8,64,2048]{2,1,0:T(8,128)(2,1)}, bf16[192,2048]{1,0:T(8,128)(2,1)}, bf16[192,2048]{1,0:T(8,128)(2,1)}, bf16[192,2048]{1,0:T(8,128)(2,1)}) custom-call(bf16[8,64,2048]{2,1,0:T(8,128)(2,1)} %bitcast.24, bf16[8,64,2048]{2,1,0:T(8,128)(2,1)} %bitcast.23, bf16[768,2048]{1,0:T(8,128)(2,1)} %bitcast.25, bf16[768,2048]{1,0:T(8,128)(2,1)} %bitcast.26, ...), custom_call_target="tpu_custom_call" | custom-call | tf_op jit(solution)/shard_map/pallas_call | solution.py:305
  193.6 0.0 copy-start.2
  193.6 0.0 copy-start.1
  193.6 3.0 %fusion = bf16[128,2048]{1,0:T(8,128)(2,1)} fusion(bf16[8,64,2048]{2,1,0:T(8,128)(2,1)} %get-tuple-element.8, s32[8,128]{1,0:T(8,128)} %copy-done.4), kind=kOutput, calls=%fused_computation.3 | convolution fusion | flops 268763136 | bytes 2625536 | tf_op jit(solution)/shard_map/dot_general | solution.py:341
  196.7 0.0 copy-start
  196.7 0.0 copy-done.2
  196.7 0.9 copy.19
  197.5 0.0 copy-done.1
  197.5 0.9 copy.20
  198.4 0.0 copy-done
  198.4 0.9 copy.21
  (1 shorter events, 0.0 us)
Async XLA Ops:
  0.6 5.1 %copy-start.3 = (bf16[128,2048]{1,0:T(8,128)(2,1)S(1)}, bf16[128,2048]{1,0:T(8,128)(2,1)}, u32[]{:S(2)}) copy-start(bf16[128,2048]{1,0:T(8,128)(2,1)} %param.7) | copy-start | bytes 1572868
  1.5 6.3 %copy-start.4 = (s32[8,128]{1,0:T(8,128)}, s32[8,128]{1,0:T(8,128)S(1)}, u32[]{:S(2)}) copy-start(s32[8,128]{1,0:T(8,128)S(1)} %fusion.1) | copy-start | bytes 12292
  193.6 3.0 %copy-start.2 = (bf16[192,2048]{1,0:T(8,128)(2,1)S(1)}, bf16[192,2048]{1,0:T(8,128)(2,1)}, u32[]{:S(2)}) copy-start(bf16[192,2048]{1,0:T(8,128)(2,1)} %get-tuple-element.9) | copy-start | bytes 2359300
  193.6 3.9 %copy-start.1 = (bf16[192,2048]{1,0:T(8,128)(2,1)S(1)}, bf16[192,2048]{1,0:T(8,128)(2,1)}, u32[]{:S(2)}) copy-start(bf16[192,2048]{1,0:T(8,128)(2,1)} %get-tuple-element.10) | copy-start | bytes 2359300
  196.7 1.8 copy-start

commit v2 on v1

--- a/solution.py
+++ b/solution.py
@@ -89,11 +89,12 @@
 
 
 def layer_kernel(
-    experts, cap, group, tok_ref, grd_ref, wg_hbm, wu_hbm, wd_hbm,
-    ret_ref, og_ref, ou_ref, od_ref,
+    experts, cap, group, all_tok, all_cot, info_ref, tok_ref, grd_ref, wg_hbm, wu_hbm, wd_hbm,
+    ret_ref, part_in, og_ref, ou_ref, od_ref,
     rows, grads, wg, wu, wd, gate, up, hid, dgate, dup, dass,
+    far_tok, far_cot, far_info, chosen, pack_tok, pack_grd, relay_in, part_out,
     core_out, core_in, x_out, x_in, own,
-    w_sem, loc_sem, tok_s, tok_r, grd_s, grd_r, ret_s, ret_r, core_s, core_r, x_s, x_r,
+    w_sem, loc_sem, far_s, far_r, tok_s, tok_r, grd_s, grd_r, ret_s, ret_r, core_s, core_r, x_s, x_r,
 ):
     me = lax.axis_index("expert")
     rank = lax.axis_index("dp")
@@ -111,34 +112,40 @@
     for c in loads:
         c.start()
     mine = [
-        pltpu.make_async_copy(tok_ref.at[me], rows.at[pl.ds(0, cap)], loc_sem.at[0]),
-        pltpu.make_async_copy(grd_ref.at[me], grads.at[pl.ds(0, cap)], loc_sem.at[1]),
+        pltpu.make_async_copy(tok_ref.at[pl.ds(0, cap)], rows.at[pl.ds(0, cap)], loc_sem.at[0]),
+        pltpu.make_async_copy(grd_ref.at[pl.ds(0, cap)], grads.at[pl.ds(0, cap)], loc_sem.at[1]),
     ]
     for c in mine:
         c.start()
 
     barrier = pltpu.get_barrier_semaphore()
-    for d in range(1, experts):
+    near = experts // 2
+    peers = list(range(1, near))
+    for d in peers + [near]:
         pl.semaphore_signal(barrier, inc=1, device_id={"expert": flip(me, d, experts)}, device_id_type=pl.DeviceIdType.MESH)
     for p in (core_peer, x_peer):
         pl.semaphore_signal(barrier, inc=1, device_id={"dp": p}, device_id_type=pl.DeviceIdType.MESH)
-    pl.semaphore_wait(barrier, experts + 1)
-
-    def to_expert(src, dst, s, r, d):
-        return pltpu.make_async_remote_copy(
-            src_ref=src, dst_ref=dst, send_sem=s.at[d], recv_sem=r.at[d],
+    pl.semaphore_wait(barrier, near + 2)
+
+    def to_expert(src, dst, s, r, at, d):
+        copy = pltpu.make_async_remote_copy(
+            src_ref=src, dst_ref=dst, send_sem=s.at[at], recv_sem=r.at[at],
             device_id={"expert": flip(me, d, experts)}, device_id_type=pl.DeviceIdType.MESH,
         )
-
-    near = list(range(1, experts // 2))
-    far = list(range(experts // 2, experts))
-    tok_c, grd_c = {}, {}
-    for d in far + near:
-        tok_c[d] = to_expert(tok_ref.at[flip(me, d, experts)], rows.at[pl.ds(d * cap, cap)], tok_s, tok_r, d)
-        tok_c[d].start()
-    for d in near + far:
-        grd_c[d] = to_expert(grd_ref.at[flip(me, d, experts)], grads.at[pl.ds(d * cap, cap)], grd_s, grd_r, d)
-        grd_c[d].start()
+        copy.start()
+        return copy
+
+    def slots(d):
+        return pl.ds(d * cap, cap)
+
+    tok_c, grd_c, ret_c = {}, {}, {}
+    info_c = to_expert(info_ref, far_info, far_s, far_r, 0, near)
+    ftok_c = to_expert(all_tok, far_tok, far_s, far_r, 1, near)
+    for q in peers:
+        tok_c[q] = to_expert(tok_ref.at[slots(q)], rows.at[slots(q)], tok_s, tok_r, q, q)
+    fcot_c = to_expert(all_cot, far_cot, far_s, far_r, 2, near)
+    for q in peers:
+        grd_c[q] = to_expert(grd_ref.at[slots(q)], grads.at[slots(q)], grd_s, grd_r, q, q)
 
     tile = ff // 2
 
@@ -189,29 +196,60 @@
             cols = pl.ds(pl.multiple_of(t * wide, wide), wide)
             store(cols, jnp.dot(left[part, :], right[:, cols], preferred_element_type=f32))
 
+    count = all_tok.shape[0]
+
+    def picks(q):
+        place = lax.broadcasted_iota(jnp.int32, (cap, count), 0).astype(f32)
+        return place == far_info[q : q + 1, :]
+
+    info_c.wait_recv()
+    for q in range(near):
+        chosen[slots(q), :] = jnp.where(picks(q), 1.0, 0.0).astype(bf16)
+    ftok_c.wait_recv()
+    for q in peers + [0]:
+        packed = jnp.dot(chosen[slots(q), :], far_tok[...], preferred_element_type=f32).astype(bf16)
+        if q == 0:
+            rows[slots(near), :] = packed
+        else:
+            pack_tok[slots(q), :] = packed
+            tok_c[near + q] = to_expert(
+                pack_tok.at[slots(q)], rows.at[slots(near + q)], tok_s, tok_r, near + q, q
+            )
     for c in loads[:2]:
         c.wait()
     mine[0].wait()
-    for d in near:
-        tok_c[d].wait_recv()
+    for q in peers:
+        tok_c[q].wait_recv()
     forward(0)
-    for d in far:
-        tok_c[d].wait_recv()
-    forward(1)
+    fcot_c.wait_recv()
+    for q in peers + [0]:
+        factor = jnp.sum(
+            jnp.where(picks(q), far_info[near + q : near + q + 1, :], 0.0), axis=1, keepdims=True
+        )
+        packed = jnp.dot(chosen[slots(q), :], far_cot[...], preferred_element_type=f32)
+        packed = (factor * packed).astype(bf16)
+        if q == 0:
+            grads[slots(near), :] = packed
+        else:
+            pack_grd[slots(q), :] = packed
+            grd_c[near + q] = to_expert(
+                pack_grd.at[slots(q)], grads.at[slots(near + q)], grd_s, grd_r, near + q, q
+            )
     loads[2].wait()
     mine[1].wait()
-    for d in near:
-        grd_c[d].wait_recv()
+    for q in peers:
+        grd_c[q].wait_recv()
     backward(0)
     assign(0)
-    ret_c = {}
-    own_back = pltpu.make_async_copy(dass.at[pl.ds(0, cap)], ret_ref.at[me], loc_sem.at[0])
+    own_back = pltpu.make_async_copy(dass.at[slots(0)], ret_ref.at[slots(0)], loc_sem.at[0])
     own_back.start()
-    for d in near:
-        ret_c[d] = to_expert(dass.at[pl.ds(d * cap, cap)], ret_ref.at[me], ret_s, ret_r, d)
-        ret_c[d].start()
-    for d in far:
-        grd_c[d].wait_recv()
+    for q in peers:
+        ret_c[q] = to_expert(dass.at[slots(q)], ret_ref.at[slots(q)], ret_s, ret_r, q, q)
+    for q in peers:
+        tok_c[near + q].wait_recv()
+    forward(1)
+    for q in peers:
+        grd_c[near + q].wait_recv()
     backward(1)
 
     core_c = {}
@@ -231,9 +269,11 @@
     for a in range(3):
         send_core(0, a, (1 - half) * 2 + (1 - side))
     assign(1)
-    for d in far:
-        ret_c[d] = to_expert(dass.at[pl.ds(d * cap, cap)], ret_ref.at[me], ret_s, ret_r, d)
-        ret_c[d].start()
+    for q in peers:
+        ret_c[near + q] = to_expert(
+            dass.at[slots(near + q)], relay_in.at[slots(q)], ret_s, ret_r, near + q, q
+        )
+    relay_in[slots(0), :] = dass[slots(near), :]
     x_c = {}
     for a in range(3):
         core_c[0, a].wait_recv()
@@ -249,6 +289,16 @@
         x_c[a].start()
     for a in range(3):
         send_core(1, a, half * 2 + (1 - side))
+    for q in peers:
+        ret_c[near + q].wait_recv()
+
+    @pl.loop(0, 4)
+    def _(t):
+        cols = pl.ds(pl.multiple_of(t * wide, wide), wide)
+        v = lax.dot_general(chosen[...], relay_in[:, cols], TN, preferred_element_type=f32)
+        part_out[:, cols] = v.astype(bf16)
+
+    part_c = to_expert(part_out, part_in, far_s, far_r, 3, near)
     for a in range(3):
         core_c[1, a].wait_recv()
 
@@ -265,8 +315,12 @@
             out[:, cols] = (own[a, :, cols] + x_in[a, :, cols].astype(f32)).astype(bf16)
 
     own_back.wait()
-    for d in range(1, experts):
-        ret_c[d].wait_recv()
+    for q in peers:
+        ret_c[q].wait_recv()
+    part_c.wait_recv()
+    for c in (info_c, ftok_c, fcot_c, part_c):
+        c.wait_send()
+    for d in tok_c:
         tok_c[d].wait_send()
         grd_c[d].wait_send()
         ret_c[d].wait_send()
@@ -284,16 +338,19 @@
     capacity = max(2, min(tok_count, 5 * tok_count * chosen // (4 * experts)))
     cap = -(-capacity // 16) * 16
     f32, bf16 = jnp.float32, jnp.bfloat16
-    hit = routes[:, :, None] == jnp.arange(experts, dtype=jnp.int32)[None, None, :]
+    near = experts // 2
+    order = jnp.arange(experts, dtype=jnp.int32) ^ lax.axis_index("expert")
+    hit = routes[:, :, None] == order[None, None, :]
     member = jnp.any(hit, axis=1)
     weight = jnp.sum(jnp.where(hit, gates[:, :, None], 0.0), axis=1)
     at = jnp.arange(tok_count, dtype=jnp.int32)
     earlier = (at[None, :] < at[:, None]).astype(bf16)
     slot = jnp.dot(earlier, member.astype(bf16), preferred_element_type=f32).astype(jnp.int32)
     slot = jnp.where(member, slot, cap)
-    picks = slot.T[:, None, :] == jnp.arange(cap, dtype=jnp.int32)[None, :, None]
-    placing = picks.reshape(experts * cap, tok_count).astype(bf16)
-    factor = jnp.sum(jnp.where(picks, weight.T[:, None, :], 0.0), axis=2).reshape(-1, 1)
+    info = jnp.concatenate([slot.T[near:].astype(f32), weight.T[near:]], axis=0)
+    picks = slot.T[:near, None, :] == jnp.arange(cap, dtype=jnp.int32)[None, :, None]
+    placing = picks.reshape(near * cap, tok_count).astype(bf16)
+    factor = jnp.sum(jnp.where(picks, weight.T[:near, None, :], 0.0), axis=2).reshape(-1, 1)
     packed = jnp.dot(placing, tokens, preferred_element_type=f32).astype(bf16)
     packed_grads = (factor * jnp.dot(placing, cotangent, preferred_element_type=f32)).astype(bf16)
     group = experts * cap // 2
@@ -302,12 +359,15 @@
     vm = pl.BlockSpec(memory_space=pltpu.VMEM)
     anyspec = pl.BlockSpec(memory_space=pl.ANY)
     sem = pltpu.SemaphoreType.DMA
-    back, grad_gate, grad_up, grad_down = pl.pallas_call(
+    back, part, grad_gate, grad_up, grad_down = pl.pallas_call(
         functools.partial(layer_kernel, experts, cap, group),
-        out_shape=[jax.ShapeDtypeStruct((experts, cap, feature), bf16)]
+        out_shape=[
+            jax.ShapeDtypeStruct((near * cap, feature), bf16),
+            jax.ShapeDtypeStruct((tok_count, feature), bf16),
+        ]
         + [jax.ShapeDtypeStruct((share, feature), bf16)] * 3,
-        in_specs=[vm, vm, anyspec, anyspec, anyspec],
-        out_specs=[vm] * 4,
+        in_specs=[vm, vm, vm, vm, vm, anyspec, anyspec, anyspec],
+        out_specs=[vm] * 5,
         scratch_shapes=[
             pltpu.VMEM((rows, feature), bf16),
             pltpu.VMEM((rows, feature), bf16),
@@ -320,12 +380,20 @@
             pltpu.VMEM((ff, rows), bf16),
             pltpu.VMEM((ff, rows), bf16),
             pltpu.VMEM((rows, feature), bf16),
+            pltpu.VMEM((tok_count, feature), bf16),
+            pltpu.VMEM((tok_count, feature), bf16),
+            pltpu.VMEM((experts, tok_count), f32),
+            pltpu.VMEM((near * cap, tok_count), bf16),
+            pltpu.VMEM((near * cap, feature), bf16),
+            pltpu.VMEM((near * cap, feature), bf16),
+            pltpu.VMEM((near * cap, feature), bf16),
+            pltpu.VMEM((tok_count, feature), bf16),
             pltpu.VMEM((6, share, feature), bf16),
             pltpu.VMEM((6, share, feature), bf16),
             pltpu.VMEM((3, share, feature), bf16),
             pltpu.VMEM((3, share, feature), bf16),
             pltpu.VMEM((3, share, feature), f32),
-            sem((3,)), sem((2,)),
+            sem((3,)), sem((2,)), sem((4,)), sem((4,)),
             sem((experts,)), sem((experts,)), sem((experts,)), sem((experts,)),
             sem((experts,)), sem((experts,)),
             sem((6,)), sem((6,)), sem((3,)), sem((3,)),
@@ -334,13 +402,11 @@
             collective_id=0, has_side_effects=True, vmem_limit_bytes=64 * 1024 * 1024 - 65536
         ),
     )(
-        packed.reshape(experts, cap, feature),
-        packed_grads.reshape(experts, cap, feature),
+        tokens, cotangent, info, packed, packed_grads,
         gate_proj[0], up_proj[0], down_proj[0],
     )
-    grad_tokens = lax.dot_general(
-        placing, back.reshape(rows, feature), TN, preferred_element_type=f32
-    ).astype(bf16)
+    grad_tokens = lax.dot_general(placing, back, TN, preferred_element_type=f32)
+    grad_tokens = (grad_tokens + part.astype(f32)).astype(bf16)
     return grad_tokens, grad_gate[None], grad_up[None], grad_down[None]
 
 

time: 200 us -> 154 us (0.77)
  the two profiles are of different devices: /device:TPU:8 before, /device:TPU:0 now
where the time goes in v2:
time: 154 us
  Pallas kernels  140 us (91%)
  matrix products  7.75 us (5%)
  local copies, waits for them, and re-layouts  2.83 us (2%)
  other arithmetic  2.38 us (2%)
    pallas_call x1, Pallas kernels, gathered(): pl.pallas_call(functools.partial(layer_kernel, experts, cap, group), out_...  140 us

profile of v2, /device:TPU:0, one launch (start us, length us, event | category | flops | bytes accessed | tf_op | source)
XLA Modules:
  0.0 153.5 jit_solution(4569117884463990157)
XLA Ops:
  0.6 0.8 compare_reduce_fusion
  1.4 0.1 eq.43
  1.5 0.1 fusion.2
  1.6 0.8 fusion.3
  2.4 0.1 select_reduce_fusion
  2.5 0.1 mul.10
  2.6 0.6 pad_maximum_fusion.info_ref
  3.2 0.1 bitcast_compare_fusion
  3.3 0.0 copy-start.3
  3.4 2.5 %fusion.grd_ref = bf16[256,2048]{1,0:T(8,128)(2,1)} fusion(pred[256,128]{1,0:T(32,128)(4,1)S(1)} %bitcast_compare_fusion, bf16[128,2048]{1,0:T(8,128)(2,1)} %all_cot.1, f32[256]{0:T(256)S(1)} %mul.10), kind=kOutput, calls=%fused_computation.2 | convolution fusion | flops 135266304 | bytes 1606656 | tf_op jit(solution)/shard_map/dot_general | solution.py:355
  5.9 0.0 copy-done.3
  5.9 2.5 %convolution_convert_fusion.tok_ref = bf16[256,2048]{1,0:T(8,128)(2,1)} fusion(pred[256,128]{1,0:T(32,128)(4,1)S(1)} %bitcast_compare_fusion, bf16[128,2048]{1,0:T(8,128)(2,1)} %all_tok.1), kind=kOutput, calls=%fused_computation.1 | convolution fusion | flops 134742016 | bytes 1605632 | tf_op jit(solution)/shard_map/dot_general | solution.py:354
  8.3 139.9 %shard_map.102 = (bf16[256,2048]{1,0:T(8,128)(2,1)}, bf16[128,2048]{1,0:T(8,128)(2,1)}, bf16[192,2048]{1,0:T(8,128)(2,1)}, bf16[192,2048]{1,0:T(8,128)(2,1)}, bf16[192,2048]{1,0:T(8,128)(2,1)}) custom-call(bf16[128,2048]{1,0:T(8,128)(2,1)} %all_tok.1, bf16[128,2048]{1,0:T(8,128)(2,1)} %all_cot.1, f32[8,128]{1,0:T(8,128)} %pad_maximum_fusion.info_ref, ...), custom_call_target="tpu_custom_call" | custom-call | tf_op jit(solution)/shard_map/pallas_call | solution.py:362
  148.2 0.0 copy-start.2
  148.2 0.0 copy-start.1
  148.3 2.6 %fusion.1 = bf16[128,2048]{1,0:T(8,128)(2,1)} fusion(pred[256,128]{1,0:T(32,128)(4,1)} %copy-done.3, bf16[256,2048]{1,0:T(8,128)(2,1)} %get-tuple-element.9, bf16[128,2048]{1,0:T(8,128)(2,1)} %get-tuple-element.10), kind=kOutput, calls=%fused_computation.4 | convolution fusion | flops 135004160 | bytes 2129920 | tf_op jit(solution)/shard_map/dot_general | solution.py:408
  150.9 0.0 copy-done.2
  150.9 0.0 copy-start
  150.9 0.9 copy.20
  151.8 0.0 copy-done.1
  151.8 0.9 copy.21
  152.7 0.0 copy-done
  152.7 0.9 copy.22
  (4 shorter events, 0.0 us)
Async XLA Ops:
  3.3 2.5 %copy-start.3 = (pred[256,128]{1,0:T(32,128)(4,1)}, pred[256,128]{1,0:T(32,128)(4,1)S(1)}, u32[]{:S(2)}) copy-start(pred[256,128]{1,0:T(32,128)(4,1)S(1)} %bitcast_compare_fusion) | copy-start | bytes 98308
  148.2 2.7 %copy-start.2 = (bf16[192,2048]{1,0:T(8,128)(2,1)S(1)}, bf16[192,2048]{1,0:T(8,128)(2,1)}, u32[]{:S(2)}) copy-start(bf16[192,2048]{1,0:T(8,128)(2,1)} %get-tuple-element.11) | copy-start | bytes 2359300
  148.2 3.5 %copy-start.1 = (bf16[192,2048]{1,0:T(8,128)(2,1)S(1)}, bf16[192,2048]{1,0:T(8,128)(2,1)}, u32[]{:S(2)}) copy-start(bf16[192,2048]{1,0:T(8,128)(2,1)} %get-tuple-element.12) | copy-start | bytes 2359300
  150.9 1.8 %copy-start = (bf16[192,2048]{1,0:T(8,128)(2,1)S(1)}, bf16[192,2048]{1,0:T(8,128)(2,1)}, u32[]{:S(2)}) copy-start(bf16[192,2048]{1,0:T(8,128)(2,1)} %get-tuple-element.13) | copy-start | bytes 2359300

commit v3 on v2

--- a/solution.py
+++ b/solution.py
@@ -89,10 +89,10 @@
 
 
 def layer_kernel(
-    experts, cap, group, all_tok, all_cot, info_ref, tok_ref, grd_ref, wg_hbm, wu_hbm, wd_hbm,
+    experts, cap, group, all_tok, all_cot, info_ref, wg_hbm, wu_hbm, wd_hbm,
     ret_ref, part_in, og_ref, ou_ref, od_ref,
     rows, grads, wg, wu, wd, gate, up, hid, dgate, dup, dass,
-    far_tok, far_cot, far_info, chosen, pack_tok, pack_grd, relay_in, part_out,
+    far_tok, far_cot, far_info, chosen, mine, near_tok, near_grd, pack_tok, pack_grd, relay_in, part_out,
     core_out, core_in, x_out, x_in, own,
     w_sem, loc_sem, far_s, far_r, tok_s, tok_r, grd_s, grd_r, ret_s, ret_r, core_s, core_r, x_s, x_r,
 ):
@@ -111,13 +111,6 @@
     ]
     for c in loads:
         c.start()
-    mine = [
-        pltpu.make_async_copy(tok_ref.at[pl.ds(0, cap)], rows.at[pl.ds(0, cap)], loc_sem.at[0]),
-        pltpu.make_async_copy(grd_ref.at[pl.ds(0, cap)], grads.at[pl.ds(0, cap)], loc_sem.at[1]),
-    ]
-    for c in mine:
-        c.start()
-
     barrier = pltpu.get_barrier_semaphore()
     near = experts // 2
     peers = list(range(1, near))
@@ -138,14 +131,69 @@
     def slots(d):
         return pl.ds(d * cap, cap)
 
-    tok_c, grd_c, ret_c = {}, {}, {}
+    tok_c, grd_c, ret_c, fcot_c = {}, {}, {}, {}
+    count = all_tok.shape[0]
+    wide = feature // 4
+    steps = range(4)
+
+    def columns(t):
+        return pl.ds(t * wide, wide)
+
+    def picks(table, q):
+        place = lax.broadcasted_iota(jnp.int32, (cap, count), 0).astype(f32)
+        return place == table[q : q + 1, :]
+
+    def factors(table, first, weights):
+        return jnp.concatenate(
+            [
+                jnp.sum(
+                    jnp.where(picks(table, first + q), table[weights + q : weights + q + 1, :], 0.0),
+                    axis=1,
+                    keepdims=True,
+                )
+                for q in range(near)
+            ],
+            axis=0,
+        )
+
+    def far_send(t):
+        fcot_c[t] = to_expert(
+            all_cot.at[:, columns(t)], far_cot.at[:, columns(t)], far_s, far_r, 3 + t, near
+        )
+
+    def grad_send(source, base, t):
+        for q in peers:
+            grd_c[base + q, t] = to_expert(
+                source.at[slots(q), columns(t)], grads.at[slots(base + q), columns(t)],
+                grd_s, grd_r, (base + q) * 4 + t, q,
+            )
+
+    def pack_grads(sel, factor, source, out, base, t):
+        v = jnp.dot(sel[...], source[:, columns(t)], preferred_element_type=f32)
+        v = (factor * v).astype(bf16)
+        out[:, columns(t)] = v
+        grads[slots(base), columns(t)] = v[:cap]
+
+    def pack_tokens(sel, source, out, base):
+        for t in steps:
+            v = jnp.dot(sel[...], source[:, columns(t)], preferred_element_type=f32).astype(bf16)
+            out[:, columns(t)] = v
+            rows[slots(base), columns(t)] = v[:cap]
+        for q in peers:
+            tok_c[base + q] = to_expert(
+                out.at[slots(q)], rows.at[slots(base + q)], tok_s, tok_r, base + q, q
+            )
+
     info_c = to_expert(info_ref, far_info, far_s, far_r, 0, near)
     ftok_c = to_expert(all_tok, far_tok, far_s, far_r, 1, near)
-    for q in peers:
-        tok_c[q] = to_expert(tok_ref.at[slots(q)], rows.at[slots(q)], tok_s, tok_r, q, q)
-    fcot_c = to_expert(all_cot, far_cot, far_s, far_r, 2, near)
-    for q in peers:
-        grd_c[q] = to_expert(grd_ref.at[slots(q)], grads.at[slots(q)], grd_s, grd_r, q, q)
+    for q in range(near):
+        mine[slots(q), :] = jnp.where(picks(info_ref, q), 1.0, 0.0).astype(bf16)
+    pack_tokens(mine, all_tok, near_tok, 0)
+    far_send(0)
+    far_send(1)
+    near_factor = factors(info_ref, 0, experts)
+    for t in steps:
+        pack_grads(mine, near_factor, all_cot, near_grd, 0, t)
 
     tile = ff // 2
 
@@ -174,8 +222,6 @@
             dup[part, span] = (dh * (gp * s)).astype(bf16)
             dgate[part, span] = (dh * up[part, span] * s * (1.0 + gp * (1.0 - s))).astype(bf16)
 
-    wide = feature // 4
-
     def assign(g):
         span = pl.ds(g * group, group)
 
@@ -196,63 +242,74 @@
             cols = pl.ds(pl.multiple_of(t * wide, wide), wide)
             store(cols, jnp.dot(left[part, :], right[:, cols], preferred_element_type=f32))
 
-    count = all_tok.shape[0]
-
-    def picks(q):
-        place = lax.broadcasted_iota(jnp.int32, (cap, count), 0).astype(f32)
-        return place == far_info[q : q + 1, :]
-
     info_c.wait_recv()
     for q in range(near):
-        chosen[slots(q), :] = jnp.where(picks(q), 1.0, 0.0).astype(bf16)
+        chosen[slots(q), :] = jnp.where(picks(far_info, near + q), 1.0, 0.0).astype(bf16)
+    far_factor = factors(far_info, near, experts + near)
     ftok_c.wait_recv()
-    for q in peers + [0]:
-        packed = jnp.dot(chosen[slots(q), :], far_tok[...], preferred_element_type=f32).astype(bf16)
-        if q == 0:
-            rows[slots(near), :] = packed
-        else:
-            pack_tok[slots(q), :] = packed
-            tok_c[near + q] = to_expert(
-                pack_tok.at[slots(q)], rows.at[slots(near + q)], tok_s, tok_r, near + q, q
-            )
+    pack_tokens(chosen, far_tok, pack_tok, near)
+    grad_send(near_grd, 0, 0)
+    far_send(2)
+    grad_send(near_grd, 0, 1)
+    far_send(3)
     for c in loads[:2]:
         c.wait()
-    mine[0].wait()
     for q in peers:
         tok_c[q].wait_recv()
     forward(0)
-    fcot_c.wait_recv()
-    for q in peers + [0]:
-        factor = jnp.sum(
-            jnp.where(picks(q), far_info[near + q : near + q + 1, :], 0.0), axis=1, keepdims=True
-        )
-        packed = jnp.dot(chosen[slots(q), :], far_cot[...], preferred_element_type=f32)
-        packed = (factor * packed).astype(bf16)
-        if q == 0:
-            grads[slots(near), :] = packed
-        else:
-            pack_grd[slots(q), :] = packed
-            grd_c[near + q] = to_expert(
-                pack_grd.at[slots(q)], grads.at[slots(near + q)], grd_s, grd_r, near + q, q
-            )
-    loads[2].wait()
-    mine[1].wait()
-    for q in peers:
-        grd_c[q].wait_recv()
-    backward(0)
-    assign(0)
-    own_back = pltpu.make_async_copy(dass.at[slots(0)], ret_ref.at[slots(0)], loc_sem.at[0])
-    own_back.start()
-    for q in peers:
-        ret_c[q] = to_expert(dass.at[slots(q)], ret_ref.at[slots(q)], ret_s, ret_r, q, q)
+
+    def relay(t):
+        fcot_c[t].wait_recv()
+        pack_grads(chosen, far_factor, far_cot, pack_grd, near, t)
+        grad_send(pack_grd, near, t)
+
+    core_c, x_c = {}, {}
+
+    def piece(j, t):
+        part = pl.ds(pl.multiple_of(j * share, share), share)
+        return jnp.dot(hid[part, :], grads[:, columns(t)], preferred_element_type=f32)
+
+    def down_core(t):
+        for d in (*peers, *(near + q for q in peers)):
+            grd_c[d, t].wait_recv()
+        core_out[2, :, columns(t)] = piece((1 - half) * 2 + (1 - side), t).astype(bf16)
+        core_c[2, t] = pltpu.make_async_remote_copy(
+            src_ref=core_out.at[2, :, columns(t)], dst_ref=core_in.at[2, :, columns(t)],
+            send_sem=core_s.at[6 + t], recv_sem=core_r.at[6 + t],
+            device_id={"dp": core_peer}, device_id_type=pl.DeviceIdType.MESH,
+        )
+        core_c[2, t].start()
+
+    def down_x(t):
+        v = piece((1 - half) * 2 + side, t)
+        core_c[2, t].wait_recv()
+        x_out[2, :, columns(t)] = (v + core_in[2, :, columns(t)].astype(f32)).astype(bf16)
+        x_c[2, t] = pltpu.make_async_remote_copy(
+            src_ref=x_out.at[2, :, columns(t)], dst_ref=x_in.at[2, :, columns(t)],
+            send_sem=x_s.at[3 + t], recv_sem=x_r.at[3 + t],
+            device_id={"dp": x_peer}, device_id_type=pl.DeviceIdType.MESH,
+        )
+        x_c[2, t].start()
+
+    relay(0)
+    grad_send(near_grd, 0, 2)
+    grad_send(near_grd, 0, 3)
+    relay(1)
     for q in peers:
         tok_c[near + q].wait_recv()
     forward(1)
-    for q in peers:
-        grd_c[near + q].wait_recv()
+    relay(2)
+    down_core(0)
+    relay(3)
+    down_core(1)
+    down_x(0)
+    down_core(2)
+    down_x(1)
+    loads[2].wait()
+    down_core(3)
+    down_x(2)
+    backward(0)
     backward(1)
-
-    core_c = {}
 
     def send_core(k, a, j):
         def store(cols, v):
@@ -266,16 +323,21 @@
         )
         core_c[k, a].start()
 
-    for a in range(3):
+    for a in range(2):
         send_core(0, a, (1 - half) * 2 + (1 - side))
+    down_x(3)
+    assign(0)
+    own_back = pltpu.make_async_copy(dass.at[slots(0)], ret_ref.at[slots(0)], loc_sem.at[0])
+    own_back.start()
     assign(1)
     for q in peers:
         ret_c[near + q] = to_expert(
             dass.at[slots(near + q)], relay_in.at[slots(q)], ret_s, ret_r, near + q, q
         )
+    for q in peers:
+        ret_c[q] = to_expert(dass.at[slots(q)], ret_ref.at[slots(q)], ret_s, ret_r, q, q)
     relay_in[slots(0), :] = dass[slots(near), :]
-    x_c = {}
-    for a in range(3):
+    for a in range(2):
         core_c[0, a].wait_recv()
 
         def store(cols, v, a=a):
@@ -298,7 +360,7 @@
         v = lax.dot_general(chosen[...], relay_in[:, cols], TN, preferred_element_type=f32)
         part_out[:, cols] = v.astype(bf16)
 
-    part_c = to_expert(part_out, part_in, far_s, far_r, 3, near)
+    part_c = to_expert(part_out, part_in, far_s, far_r, 2, near)
     for a in range(3):
         core_c[1, a].wait_recv()
 
@@ -307,7 +369,8 @@
 
         weight_grad(a, half * 2 + side, store)
     for a, out in enumerate((og_ref, ou_ref, od_ref)):
-        x_c[a].wait_recv()
+        for key in [k for k in x_c if k == a or (a == 2 and isinstance(k, tuple))]:
+            x_c[key].wait_recv()
 
         @pl.loop(0, 4)
         def _(t, a=a, out=out):
@@ -318,11 +381,10 @@
     for q in peers:
         ret_c[q].wait_recv()
     part_c.wait_recv()
-    for c in (info_c, ftok_c, fcot_c, part_c):
+    for c in (info_c, ftok_c, part_c, *fcot_c.values(), *grd_c.values()):
         c.wait_send()
     for d in tok_c:
         tok_c[d].wait_send()
-        grd_c[d].wait_send()
         ret_c[d].wait_send()
     for c in core_c.values():
         c.wait_send()
@@ -347,12 +409,9 @@
     earlier = (at[None, :] < at[:, None]).astype(bf16)
     slot = jnp.dot(earlier, member.astype(bf16), preferred_element_type=f32).astype(jnp.int32)
     slot = jnp.where(member, slot, cap)
-    info = jnp.concatenate([slot.T[near:].astype(f32), weight.T[near:]], axis=0)
+    info = jnp.concatenate([slot.T.astype(f32), weight.T], axis=0)
     picks = slot.T[:near, None, :] == jnp.arange(cap, dtype=jnp.int32)[None, :, None]
     placing = picks.reshape(near * cap, tok_count).astype(bf16)
-    factor = jnp.sum(jnp.where(picks, weight.T[:near, None, :], 0.0), axis=2).reshape(-1, 1)
-    packed = jnp.dot(placing, tokens, preferred_element_type=f32).astype(bf16)
-    packed_grads = (factor * jnp.dot(placing, cotangent, preferred_element_type=f32)).astype(bf16)
     group = experts * cap // 2
     share = ff // 4
     rows = experts * cap
@@ -366,7 +425,7 @@
             jax.ShapeDtypeStruct((tok_count, feature), bf16),
         ]
         + [jax.ShapeDtypeStruct((share, feature), bf16)] * 3,
-        in_specs=[vm, vm, vm, vm, vm, anyspec, anyspec, anyspec],
+        in_specs=[vm, vm, vm, anyspec, anyspec, anyspec],
         out_specs=[vm] * 5,
         scratch_shapes=[
             pltpu.VMEM((rows, feature), bf16),
@@ -382,8 +441,11 @@
             pltpu.VMEM((rows, feature), bf16),
             pltpu.VMEM((tok_count, feature), bf16),
             pltpu.VMEM((tok_count, feature), bf16),
-            pltpu.VMEM((experts, tok_count), f32),
+            pltpu.VMEM((2 * experts, tok_count), f32),
             pltpu.VMEM((near * cap, tok_count), bf16),
+            pltpu.VMEM((near * cap, tok_count), bf16),
+            pltpu.VMEM((near * cap, feature), bf16),
+            pltpu.VMEM((near * cap, feature), bf16),
             pltpu.VMEM((near * cap, feature), bf16),
             pltpu.VMEM((near * cap, feature), bf16),
             pltpu.VMEM((near * cap, feature), bf16),
@@ -393,16 +455,16 @@
             pltpu.VMEM((3, share, feature), bf16),
             pltpu.VMEM((3, share, feature), bf16),
             pltpu.VMEM((3, share, feature), f32),
-            sem((3,)), sem((2,)), sem((4,)), sem((4,)),
-            sem((experts,)), sem((experts,)), sem((experts,)), sem((experts,)),
+            sem((3,)), sem((1,)), sem((7,)), sem((7,)),
+            sem((experts,)), sem((experts,)), sem((experts * 4,)), sem((experts * 4,)),
             sem((experts,)), sem((experts,)),
-            sem((6,)), sem((6,)), sem((3,)), sem((3,)),
+            sem((10,)), sem((10,)), sem((7,)), sem((7,)),
         ],
         compiler_params=pltpu.CompilerParams(
             collective_id=0, has_side_effects=True, vmem_limit_bytes=64 * 1024 * 1024 - 65536
         ),
     )(
-        tokens, cotangent, info, packed, packed_grads,
+        tokens, cotangent, info,
         gate_proj[0], up_proj[0], down_proj[0],
     )
     grad_tokens = lax.dot_general(placing, back, TN, preferred_element_type=f32)

time: 154 us -> 138 us (0.90)
  Pallas kernels: 140 us -> 128 us
  matrix products: 7.75 us -> 2.77 us
    pallas_call x1, Pallas kernels: 140 us -> 128 us  [gathered(): pl.pallas_call(functools.partial(layer_kernel, experts, cap, group), out_...]
    dot_general x2 -> x0, matrix products: 4.97 us -> none  [the longest x1 2.52 us: gathered(): jnp.dot(placing, cotangent, preferred_element_type=f32)]
    unnamed x11 -> x7, local copies, waits for them, and re-layouts: 2.66 us -> 3.85 us
where the time goes in v3:
time: 138 us
  Pallas kernels  128 us (93%)
  local copies, waits for them, and re-layouts  3.94 us (3%)
  other arithmetic  2.87 us (2%)
  matrix products  2.77 us (2%)
    pallas_call x1, Pallas kernels, gathered(): pl.pallas_call(functools.partial(layer_kernel, experts, cap, group), out_...  128 us
    unnamed x7, local copies, waits for them, and re-layouts  3.85 us

profile of v3, /device:TPU:0, one launch (start us, length us, event | category | flops | bytes accessed | tf_op | source)
XLA Modules:
  0.0 138.1 jit_solution(6413975386001934060)
XLA Ops:
  0.6 0.8 compare_reduce_fusion
  1.4 0.1 eq.39
  1.5 0.8 fusion.2
  2.3 0.1 fusion.3
  2.4 0.6 pad_maximum_fusion.info_ref
  3.0 0.7 bitcast_compare_fusion
  3.7 127.9 %shard_map.102 = (bf16[256,2048]{1,0:T(8,128)(2,1)}, bf16[128,2048]{1,0:T(8,128)(2,1)}, bf16[192,2048]{1,0:T(8,128)(2,1)}, bf16[192,2048]{1,0:T(8,128)(2,1)}, bf16[192,2048]{1,0:T(8,128)(2,1)}) custom-call(bf16[128,2048]{1,0:T(8,128)(2,1)} %all_tok.1, bf16[128,2048]{1,0:T(8,128)(2,1)} %all_cot.1, f32[16,128]{1,0:T(8,128)} %pad_maximum_fusion.info_ref, ...), custom_call_target="tpu_custom_call" | custom-call | tf_op jit(solution)/shard_map/pallas_call | solution.py:421
  131.6 0.0 copy-start.1
  131.6 0.0 copy-start
  131.6 2.6 %fusion = bf16[128,2048]{1,0:T(8,128)(2,1)} fusion(pred[256,128]{1,0:T(32,128)(4,1)} %bitcast_compare_fusion, bf16[256,2048]{1,0:T(8,128)(2,1)} %get-tuple-element.9, bf16[128,2048]{1,0:T(8,128)(2,1)} %get-tuple-element.10), kind=kOutput, calls=%fused_computation.1 | convolution fusion | flops 135004160 | bytes 2129920 | tf_op jit(solution)/shard_map/dot_general | solution.py:470
  134.3 2.1 %copy.18 = bf16[1,192,2048]{2,1,0:T(8,128)(2,1)} copy(bf16[1,192,2048]{2,1,0:T(8,128)(2,1)} %bitcast.19) | data formatting | bytes 1572864
  136.4 0.0 copy-done.1
  136.4 0.9 copy.19
  137.2 0.0 copy-done
  137.2 0.9 copy.20
  (3 shorter events, 0.0 us)
Async XLA Ops:
  131.6 4.7 %copy-start.1 = (bf16[192,2048]{1,0:T(8,128)(2,1)S(1)}, bf16[192,2048]{1,0:T(8,128)(2,1)}, u32[]{:S(2)}) copy-start(bf16[192,2048]{1,0:T(8,128)(2,1)} %get-tuple-element.12) | copy-start | bytes 2359300
  131.6 5.6 %copy-start = (bf16[192,2048]{1,0:T(8,128)(2,1)S(1)}, bf16[192,2048]{1,0:T(8,128)(2,1)}, u32[]{:S(2)}) copy-start(bf16[192,2048]{1,0:T(8,128)(2,1)} %get-tuple-element.13) | copy-start | bytes 2359300

commit v4 on v3

--- a/solution.py
+++ b/solution.py
@@ -90,9 +90,9 @@
 
 def layer_kernel(
     experts, cap, group, all_tok, all_cot, info_ref, wg_hbm, wu_hbm, wd_hbm,
-    ret_ref, part_in, og_ref, ou_ref, od_ref,
+    ot_ref, og_ref, ou_ref, od_ref,
     rows, grads, wg, wu, wd, gate, up, hid, dgate, dup, dass,
-    far_tok, far_cot, far_info, chosen, mine, near_tok, near_grd, pack_tok, pack_grd, relay_in, part_out,
+    far_tok, far_cot, far_info, chosen, mine, near_tok, near_grd, pack_tok, pack_grd, relay_in, part_out, ret_ref, part_in,
     core_out, core_in, x_out, x_in, own,
     w_sem, loc_sem, far_s, far_r, tok_s, tok_r, grd_s, grd_r, ret_s, ret_r, core_s, core_r, x_s, x_r,
 ):
@@ -270,8 +270,8 @@
         return jnp.dot(hid[part, :], grads[:, columns(t)], preferred_element_type=f32)
 
     def down_core(t):
-        for d in (*peers, *(near + q for q in peers)):
-            grd_c[d, t].wait_recv()
+        for q in peers:
+            grd_c[near + q, t].wait_recv()
         core_out[2, :, columns(t)] = piece((1 - half) * 2 + (1 - side), t).astype(bf16)
         core_c[2, t] = pltpu.make_async_remote_copy(
             src_ref=core_out.at[2, :, columns(t)], dst_ref=core_in.at[2, :, columns(t)],
@@ -299,16 +299,18 @@
         tok_c[near + q].wait_recv()
     forward(1)
     relay(2)
+    for q in peers:
+        for t in steps:
+            grd_c[q, t].wait_recv()
     down_core(0)
     relay(3)
     down_core(1)
     down_x(0)
+    loads[2].wait()
+    backward(0)
     down_core(2)
     down_x(1)
-    loads[2].wait()
     down_core(3)
-    down_x(2)
-    backward(0)
     backward(1)
 
     def send_core(k, a, j):
@@ -325,6 +327,7 @@
 
     for a in range(2):
         send_core(0, a, (1 - half) * 2 + (1 - side))
+    down_x(2)
     down_x(3)
     assign(0)
     own_back = pltpu.make_async_copy(dass.at[slots(0)], ret_ref.at[slots(0)], loc_sem.at[0])
@@ -368,6 +371,17 @@
             own[a, :, cols] = v + core_in[3 + a, :, cols].astype(f32)
 
         weight_grad(a, half * 2 + side, store)
+    own_back.wait()
+    for q in peers:
+        ret_c[q].wait_recv()
+    part_c.wait_recv()
+
+    @pl.loop(0, 4)
+    def _(t):
+        cols = pl.ds(pl.multiple_of(t * wide, wide), wide)
+        v = lax.dot_general(mine[...], ret_ref[:, cols], TN, preferred_element_type=f32)
+        ot_ref[:, cols] = (v + part_in[:, cols].astype(f32)).astype(bf16)
+
     for a, out in enumerate((og_ref, ou_ref, od_ref)):
         for key in [k for k in x_c if k == a or (a == 2 and isinstance(k, tuple))]:
             x_c[key].wait_recv()
@@ -377,10 +391,6 @@
             cols = pl.ds(pl.multiple_of(t * wide, wide), wide)
             out[:, cols] = (own[a, :, cols] + x_in[a, :, cols].astype(f32)).astype(bf16)
 
-    own_back.wait()
-    for q in peers:
-        ret_c[q].wait_recv()
-    part_c.wait_recv()
     for c in (info_c, ftok_c, part_c, *fcot_c.values(), *grd_c.values()):
         c.wait_send()
     for d in tok_c:
@@ -410,23 +420,20 @@
     slot = jnp.dot(earlier, member.astype(bf16), preferred_element_type=f32).astype(jnp.int32)
     slot = jnp.where(member, slot, cap)
     info = jnp.concatenate([slot.T.astype(f32), weight.T], axis=0)
-    picks = slot.T[:near, None, :] == jnp.arange(cap, dtype=jnp.int32)[None, :, None]
-    placing = picks.reshape(near * cap, tok_count).astype(bf16)
     group = experts * cap // 2
     share = ff // 4
     rows = experts * cap
     vm = pl.BlockSpec(memory_space=pltpu.VMEM)
     anyspec = pl.BlockSpec(memory_space=pl.ANY)
     sem = pltpu.SemaphoreType.DMA
-    back, part, grad_gate, grad_up, grad_down = pl.pallas_call(
+    grad_tokens, grad_gate, grad_up, grad_down = pl.pallas_call(
         functools.partial(layer_kernel, experts, cap, group),
         out_shape=[
-            jax.ShapeDtypeStruct((near * cap, feature), bf16),
             jax.ShapeDtypeStruct((tok_count, feature), bf16),
         ]
         + [jax.ShapeDtypeStruct((share, feature), bf16)] * 3,
         in_specs=[vm, vm, vm, anyspec, anyspec, anyspec],
-        out_specs=[vm] * 5,
+        out_specs=[vm] * 4,
         scratch_shapes=[
             pltpu.VMEM((rows, feature), bf16),
             pltpu.VMEM((rows, feature), bf16),
@@ -450,6 +457,8 @@
             pltpu.VMEM((near * cap, feature), bf16),
             pltpu.VMEM((near * cap, feature), bf16),
             pltpu.VMEM((tok_count, feature), bf16),
+            pltpu.VMEM((near * cap, feature), bf16),
+            pltpu.VMEM((tok_count, feature), bf16),
             pltpu.VMEM((6, share, feature), bf16),
             pltpu.VMEM((6, share, feature), bf16),
             pltpu.VMEM((3, share, feature), bf16),
@@ -467,8 +476,6 @@
         tokens, cotangent, info,
         gate_proj[0], up_proj[0], down_proj[0],
     )
-    grad_tokens = lax.dot_general(placing, back, TN, preferred_element_type=f32)
-    grad_tokens = (grad_tokens + part.astype(f32)).astype(bf16)
     return grad_tokens, grad_gate[None], grad_up[None], grad_down[None]
 
 

time: 138 us -> 137 us (level)
  matrix products: 2.77 us -> 0.14 us
  local copies, waits for them, and re-layouts: 3.94 us -> 5.85 us
    dot_general x1 -> x0, matrix products: 2.64 us -> none  [gathered(): grad_tokens = lax.dot_general(placing, back, TN, preferred_element_type=f32)]
    unnamed x7 -> x8, local copies, waits for them, and re-layouts: 3.85 us -> 5.85 us
where the time goes in v4:
time: 137 us
  Pallas kernels  128 us (93%)
  local copies, waits for them, and re-layouts  5.85 us (4%)
  other arithmetic  2.15 us (2%)
    pallas_call x1, Pallas kernels, gathered(): pl.pallas_call(functools.partial(layer_kernel, experts, cap, group), out_...  128 us
    unnamed x8, local copies, waits for them, and re-layouts  5.85 us

profile of v4, /device:TPU:0, one launch (start us, length us, event | category | flops | bytes accessed | tf_op | source)
XLA Modules:
  0.0 136.7 jit_solution(6423629475324595304)
XLA Ops:
  0.6 0.8 compare_reduce_fusion
  1.4 0.1 fusion.1
  1.5 0.8 fusion.2
  2.3 0.6 pad_maximum_fusion.info_ref
  2.9 127.9 %shard_map.102 = (bf16[128,2048]{1,0:T(8,128)(2,1)}, bf16[192,2048]{1,0:T(8,128)(2,1)}, bf16[192,2048]{1,0:T(8,128)(2,1)}, bf16[192,2048]{1,0:T(8,128)(2,1)}) custom-call(bf16[128,2048]{1,0:T(8,128)(2,1)} %all_tok.1, bf16[128,2048]{1,0:T(8,128)(2,1)} %all_cot.1, f32[16,128]{1,0:T(8,128)} %pad_maximum_fusion.info_ref, bf16[768,2048]{1,0:T(8,128)(2,1)} %bitcast.10, ...), custom_call_target="tpu_custom_call" | custom-call | tf_op jit(solution)/shard_map/pallas_call | solution.py:429
  130.8 0.0 copy-start.1
  130.9 0.0 copy-start
  130.9 2.0 %copy.17 = bf16[128,2048]{1,0:T(8,128)(2,1)} copy(bf16[128,2048]{1,0:T(8,128)(2,1)} %get-tuple-element.16) | data formatting | bytes 1048576
  132.9 2.1 %copy.18 = bf16[1,192,2048]{2,1,0:T(8,128)(2,1)} copy(bf16[1,192,2048]{2,1,0:T(8,128)(2,1)} %bitcast.15) | data formatting | bytes 1572864
  135.0 0.0 copy-done.1
  135.0 0.9 copy.19
  135.8 0.0 copy-done
  135.8 0.9 copy.20
  (1 shorter events, 0.0 us)
Async XLA Ops:
  130.8 4.1 %copy-start.1 = (bf16[192,2048]{1,0:T(8,128)(2,1)S(1)}, bf16[192,2048]{1,0:T(8,128)(2,1)}, u32[]{:S(2)}) copy-start(bf16[192,2048]{1,0:T(8,128)(2,1)} %get-tuple-element.10) | copy-start | bytes 2359300
  130.9 5.0 %copy-start = (bf16[192,2048]{1,0:T(8,128)(2,1)S(1)}, bf16[192,2048]{1,0:T(8,128)(2,1)}, u32[]{:S(2)}) copy-start(bf16[192,2048]{1,0:T(8,128)(2,1)} %get-tuple-element.11) | copy-start | bytes 2359300
